TPU v7x, 512 devices: a whole 4x8x8 slice. The times are simulated.
512 devices in a mesh: shard: 128 (over y, z_hi, x), tensor: 4 (over z_lo, core).
Axes of the slice: x: 4, y: 8, z: 8 (z_hi: 4, z_lo: 2; z = z_hi * 2 + z_lo), core: 2. Of those that a mesh axis runs over, the one named last changes fastest.
Arguments:
- gradients: bfloat16 [128, 128, 32, 512], P('shard', None, 'tensor'), may hold values from -2 to 2
- master_weights: float32 [128, 32, 512], P('shard', 'tensor'), may hold values from -6 to 6
- first_moment: float32 [128, 32, 512], P('shard', 'tensor'), may hold values from -4 to 4
- second_moment: float32 [128, 32, 512], P('shard', 'tensor'), may hold values from 0.5 to 4
- old_basis: float32 [128, 512, 512], P('shard', 'tensor')
- old_stats: float32 [128, 512, 512], P('shard', 'tensor'), as said below
- owner_table: int32 [128], replicated, may hold values from 0 to 127, each once
Outputs:
- updated_weights: float32 [128, 32, 512], P(None, 'tensor')
- new_first: float32 [128, 32, 512], P('shard', 'tensor')
- new_second: float32 [128, 32, 512], P('shard', 'tensor')
- new_basis: float32 [128, 512, 512], P('shard', 'tensor')
- new_stats: float32 [128, 512, 512], P('shard', 'tensor')
Inputs may be any that keep to these rules, and one draw needn't show every extreme that they name: owner_table names every owner 0 to 127 exactly once. `old_stats`: each block's matrix is symmetric.
All inputs are finite; a program needn't handle non-finite values.
Results may differ from a plain program's by a relative error of at most 0.004.
Values may be sent and summed in bfloat16 or wider, within the bound.
No kernel may reach another device: no remote copies, remote signals or barrier semaphores. Data moves between devices by JAX's collectives and lax.ppermute only.
A program may use at most 64 MiB of HBM per device.

v0:
```python
import jax
import jax.numpy as jnp
from jax import lax
from jax.sharding import PartitionSpec as P

NS_ITERS = 3
momentum_decay = 0.9
square_decay = 0.95
stats_decay = 0.95
step_size = 0.05
start_gain = 1.7
epsilon = 1e-06


def gram_of(matrix):
    return lax.dot_general(
        matrix, matrix, (((0,), (0,)), ((), ())), precision=lax.Precision.HIGHEST
    )


def body(gradients, master_weights, first_moment, second_moment, old_basis, old_stats, owner_table):
    highest = lax.Precision.HIGHEST
    blocks = owner_table.shape[0]
    places = jnp.arange(blocks, dtype=jnp.int32)
    inverse = jnp.sum(
        jnp.where(owner_table[None, :] == places[:, None], places[None, :], 0), axis=1
    )
    ordered = jnp.take(gradients[0], inverse, axis=0)
    summed = lax.psum_scatter(
        ordered.astype(jnp.float32), "shard", scatter_dimension=0, tiled=True
    )[0]
    whole_basis = lax.all_gather(old_basis[0], "tensor", axis=0, tiled=True)
    turned = jnp.dot(summed, whole_basis, precision=highest)
    first_new = momentum_decay * first_moment[0] + (1.0 - momentum_decay) * turned
    second_new = square_decay * second_moment[0] + (1.0 - square_decay) * turned * turned
    direction = first_new / jnp.sqrt(second_new)
    rotated_back = lax.dot_general(
        direction, whole_basis, (((1,), (1,)), ((), ())), precision=highest
    )
    weight_new = master_weights[0] - step_size * rotated_back
    gathered = lax.all_gather(weight_new[None], "shard", axis=0, tiled=True)
    updated_weights = jnp.take(gathered, owner_table, axis=0)
    rows_here = old_basis.shape[1]
    position = lax.axis_index("tensor") * rows_here
    whole_grad = lax.all_gather(summed, "tensor", axis=0, tiled=True)
    own_columns = lax.dynamic_slice_in_dim(whole_grad, position, rows_here, 1)
    fresh_term = lax.dot_general(
        own_columns, whole_grad, (((0,), (0,)), ((), ())), precision=highest
    )
    stats_new = stats_decay * old_stats[0] + (1.0 - stats_decay) * fresh_term
    power_part = jnp.dot(stats_new, whole_basis, precision=highest)
    whole_power = lax.all_gather(power_part, "tensor", axis=0, tiled=True)
    gram_matrix = gram_of(whole_power)
    factor = start_gain / jnp.sqrt(jnp.trace(gram_matrix) + epsilon)
    current = whole_power * factor
    gram_matrix = gram_matrix * (factor * factor)
    for sweep in range(NS_ITERS):
        if sweep > 0:
            gram_matrix = gram_of(current)
        if sweep + 1 < NS_ITERS:
            current = 1.5 * current - 0.5 * jnp.dot(current, gram_matrix, precision=highest)
        else:
            own_rows = lax.dynamic_slice_in_dim(current, position, rows_here, 0)
            current = 1.5 * own_rows - 0.5 * jnp.dot(own_rows, gram_matrix, precision=highest)
    return (updated_weights, first_new[None], second_new[None], current[None], stats_new[None])


def solution(mesh):
    return jax.shard_map(
        body,
        mesh=mesh,
        in_specs=(
            P("shard", None, "tensor", None),
            P("shard", "tensor", None),
            P("shard", "tensor", None),
            P("shard", "tensor", None),
            P("shard", "tensor", None),
            P("shard", "tensor", None),
            P(),
        ),
        out_specs=(
            P(None, "tensor", None),
            P("shard", "tensor", None),
            P("shard", "tensor", None),
            P("shard", "tensor", None),
            P("shard", "tensor", None),
        ),
        check_vma=False,
    )
```

profile of v0, /device:TPU:2, one launch (start us, length us, event | category | flops | bytes accessed | tf_op | source)
XLA Modules:
  0.0 952.9 jit_solution(6312819126764942959)
XLA Ops:
  8.0 0.0 copy-start
  8.0 0.0 reduce-scatter.2.cloned.1.call-start
  8.1 0.8 select_reduce_fusion.1
  8.9 0.3 copy-done
  9.2 0.6 gather_fusion
  9.9 0.0 copy-start.4
  9.9 1.5 select_convert_fusion
  11.5 0.0 reduce-scatter.2.cloned.1.call-update
  11.5 0.0 copy-start.5
  11.5 0.0 copy-start.6
  11.5 0.0 copy-start.8
  11.5 0.0 all-gather.9.cloned.1.call-start
  11.6 0.5 all-gather.9.cloned.1.call-update
  12.1 0.0 all-gather.7.cloned.1.call-start
  12.1 765.6 %reduce-scatter.2.cloned.1.call-done = f32[1,8,512]{2,1,0:T(8,128)} async-done(((f32[128,8,512]{2,1,0:T(8,128)}), f32[1,8,512]{2,1,0:T(8,128)}) %reduce-scatter.2.cloned.1.call-update) | async-done | bytes 16400 | tf_op jit(solution)/shard_map/reduce_scatter | solution.py:29
  777.7 0.0 copy-start.7
  777.7 5.6 all-gather.2
  783.3 0.0 copy-done.4
  783.3 0.4 fusion.2
  783.7 0.0 copy-start.3
  783.7 0.0 copy-start.9
  783.7 0.0 all-gather.9.cloned.1.call-done
  783.8 0.0 copy-start.1
  783.8 2.7 fusion.6
  786.5 0.0 all-gather.7.cloned.1.call-update
  786.5 0.0 all-gather.11.cloned.1.call-start
  786.6 0.0 copy-done.7
  786.6 0.0 copy-done.1
  786.6 0.6 fusion.9
  787.2 0.0 copy-done.5
  787.2 0.0 copy-done.6
  787.2 0.0 copy-done.8
  787.2 1.6 fusion.5
  788.8 0.0 all-gather.11.cloned.1.call-update
  788.8 0.0 copy-done.9
  788.9 0.6 fusion.24
  789.5 21.0 %all-gather.7.cloned.1.call-done = f32[512,512]{1,0:T(8,128)} async-done(((f32[128,512]{1,0:T(8,128)}), f32[512,512]{1,0:T(8,128)}) %all-gather.7.cloned.1.call-update) | async-done | bytes 1048592 | tf_op jit(solution)/shard_map/all_gather | solution.py:52
  810.5 0.0 copy-start.2
  810.5 4.1 select_reduce_fusion
  814.6 0.0 copy-done.3
  815.3 0.0 copy-done.2
  815.3 1.9 fusion.1
  817.2 1.9 fusion.33
  819.1 1.9 fusion
  820.9 1.9 fusion.34
  822.8 1.4 fusion.4
  824.2 117.3 %all-gather.11.cloned.1.call-done = f32[1024,512]{1,0:T(8,128)} async-done(((f32[8,512]{1,0:T(8,128)}), f32[1024,512]{1,0:T(8,128)}) %all-gather.11.cloned.1.call-update) | async-done | bytes 2097168 | tf_op jit(solution)/shard_map/all_gather | solution.py:41
  941.5 2.3 gather_fusion.1
  943.8 1.5 broadcast_select_fusion
  (6 shorter events, 0.0 us)
Async XLA Ops:
  8.0 1.2 copy-start
  8.0 769.7 %reduce-scatter.2.cloned.1.call-start = ((), (), s32[]{:S(2)}) async-start(), calls=%async_computation.1 | async-start | bytes 2113536 | tf_op jit(solution)/shard_map/reduce_scatter | solution.py:29
  9.9 773.4 %copy-start.4 = (f32[1,128,512]{2,1,0:T(8,128)S(1)}, f32[1,128,512]{2,1,0:T(8,128)}, u32[]{:S(2)}) copy-start(f32[1,128,512]{2,1,0:T(8,128)} %param.12) | copy-start | bytes 786436
  11.5 775.7 %copy-start.5 = (f32[1,8,512]{2,1,0:T(8,128)S(1)}, f32[1,8,512]{2,1,0:T(8,128)}, u32[]{:S(2)}) copy-start(f32[1,8,512]{2,1,0:T(8,128)} %param.9) | copy-start | bytes 49156
  11.5 775.7 %copy-start.6 = (f32[1,8,512]{2,1,0:T(8,128)S(1)}, f32[1,8,512]{2,1,0:T(8,128)}, u32[]{:S(2)}) copy-start(f32[1,8,512]{2,1,0:T(8,128)} %param.10) | copy-start | bytes 49156
  11.5 775.7 %copy-start.8 = (f32[1,8,512]{2,1,0:T(8,128)S(1)}, f32[1,8,512]{2,1,0:T(8,128)}, u32[]{:S(2)}) copy-start(f32[1,8,512]{2,1,0:T(8,128)} %param.8) | copy-start | bytes 49156
  11.5 772.2 %all-gather.9.cloned.1.call-start = ((), (), s32[]{:S(2)}) async-start(), calls=%async_computation.3 | async-start | bytes 1310720 | tf_op jit(solution)/shard_map/all_gather | solution.py:32
  12.1 798.4 %all-gather.7.cloned.1.call-start = ((), (), s32[]{:S(2)}) async-start(), calls=%async_computation.2 | async-start | bytes 1310720 | tf_op jit(solution)/shard_map/all_gather | solution.py:52
  777.7 8.9 copy-start.7
  783.7 30.9 %copy-start.3 = (f32[128,512]{1,0:T(8,128)}, f32[128,512]{1,0:T(8,128)S(1)}, u32[]{:S(2)}) copy-start(f32[128,512]{1,0:T(8,128)S(1)} %fusion.2) | copy-start | bytes 786436
  783.7 5.1 copy-start.9
  783.8 2.8 copy-start.1
  786.5 155.0 %all-gather.11.cloned.1.call-start = ((), (), s32[]{:S(2)}) async-start(), calls=%async_computation.4 | async-start | bytes 2113536 | tf_op jit(solution)/shard_map/all_gather | solution.py:41
  810.5 4.8 copy-start.2
Sparse Core Ops, SparseCore 0:
  12.2 765.4 reduce-scatter.1
Sparse Core Ops, SparseCore 1:
  14.1 30.2 all-gather.8
  786.6 23.8 all-gather.6
  815.4 126.0 all-gather.10
where the time goes:
time: 953 us
  waiting for transfers between devices  904 us (95%)
  matrix products  18.4 us (2%)
  between operations  16.6 us (2%)
    reduce_scatter x1, waiting for transfers between devices, body(): lax.psum_scatter(ordered.astype(jnp.float32), 'shard', scatter_dimension=...  766 us
    all_gather x1, waiting for transfers between devices, body(): gathered = lax.all_gather(weight_new[None], 'shard', axis=0, tiled=True)  117 us
    all_gather x1, waiting for transfers between devices, body(): whole_power = lax.all_gather(power_part, 'tensor', axis=0, tiled=True)  21 us
  transfers between devices with their start and end apart: 4, of which 3 were waited for; matrix products, arithmetic and copies ran while one was open for 2% of the time, Pallas kernels for 0%

commit v1 on v0

--- a/solution.py
+++ b/solution.py
@@ -49,7 +49,9 @@
     )
     stats_new = stats_decay * old_stats[0] + (1.0 - stats_decay) * fresh_term
     power_part = jnp.dot(stats_new, whole_basis, precision=highest)
-    whole_power = lax.all_gather(power_part, "tensor", axis=0, tiled=True)
+    whole_power = jnp.concatenate(
+        lax.all_to_all(jnp.stack([power_part] * lax.axis_size("tensor")), "tensor", 0, 0), axis=0
+    )
     gram_matrix = gram_of(whole_power)
     factor = start_gain / jnp.sqrt(jnp.trace(gram_matrix) + epsilon)
     current = whole_power * factor

time: 953 us -> 918 us (0.963)
  waiting for transfers between devices: 904 us -> 866 us
    all_gather x1, waiting for transfers between devices: 117 us -> 85.8 us  [body(): gathered = lax.all_gather(weight_new[None], 'shard', axis=0, tiled=True)]
    all_gather x1, waiting for transfers between devices: 0.03 us -> 29.4 us  [body(): whole_basis = lax.all_gather(old_basis[0], 'tensor', axis=0, tiled=True)]
    reduce_scatter x1, waiting for transfers between devices: 766 us -> 737 us  [body(): lax.psum_scatter(ordered.astype(jnp.float32), 'shard', scatter_dimension=...]
    all_gather x1 -> x0, waiting for transfers between devices: 21 us -> none  [body(): whole_power = lax.all_gather(power_part, 'tensor', axis=0, tiled=True)]
    all_to_all x0 -> x1, waiting for transfers between devices: none -> 13.8 us  [body(): lax.all_to_all(jnp.stack([power_part] * lax.axis_size('tensor')), 'tensor...]
  transfers between devices with their start and end apart: 4 -> 4, of which waited for: 3 -> 4; matrix products, arithmetic and copies ran while one was open for 2% -> 2% of each run, Pallas kernels for 0% -> 0%
where the time goes in v1:
time: 918 us
  waiting for transfers between devices  866 us (94%)
  matrix products  17.1 us (2%)
  between operations  16.4 us (2%)
    reduce_scatter x1, waiting for transfers between devices, body(): lax.psum_scatter(ordered.astype(jnp.float32), 'shard', scatter_dimension=...  737 us
    all_gather x1, waiting for transfers between devices, body(): gathered = lax.all_gather(weight_new[None], 'shard', axis=0, tiled=True)  85.8 us
    all_gather x1, waiting for transfers between devices, body(): whole_basis = lax.all_gather(old_basis[0], 'tensor', axis=0, tiled=True)  29.4 us
  transfers between devices with their start and end apart: 4, of which 4 were waited for; matrix products, arithmetic and copies ran while one was open for 2% of the time, Pallas kernels for 0%

profile of v1, /device:TPU:2, one launch (start us, length us, event | category | flops | bytes accessed | tf_op | source)
XLA Modules:
  0.0 917.7 jit_solution(13574296122828042371)
XLA Ops:
  8.0 0.0 copy-start
  8.0 0.0 all-gather.6.cloned.1.call-start
  8.1 0.7 all-gather.6.cloned.1.call-update
  8.7 0.0 reduce-scatter.2.cloned.1.call-start
  8.8 0.8 select_reduce_fusion.1
  9.6 0.0 copy-done
  9.6 0.6 gather_fusion
  10.3 1.5 select_convert_fusion
  11.8 0.0 copy-start.4
  11.8 0.0 copy-start.5
  11.8 0.0 copy-start.7
  11.8 0.0 copy-start.3
  11.8 0.0 reduce-scatter.2.cloned.1.call-update
  11.8 0.0 all-gather.8.cloned.1.call-start
  11.9 29.4 %all-gather.6.cloned.1.call-done = f32[1,512,512]{2,1,0:T(8,128)} async-done(((f32[1,128,512]{2,1,0:T(8,128)}), f32[1,512,512]{2,1,0:T(8,128)}) %all-gather.6.cloned.1.call-update) | async-done | bytes 1048592 | tf_op jit(solution)/shard_map/all_gather | solution.py:32
  41.3 0.0 copy-start.1
  41.3 736.8 %reduce-scatter.2.cloned.1.call-done = f32[1,8,512]{2,1,0:T(8,128)} async-done(((f32[128,8,512]{2,1,0:T(8,128)}), f32[1,8,512]{2,1,0:T(8,128)}) %reduce-scatter.2.cloned.1.call-update) | async-done | bytes 16400 | tf_op jit(solution)/shard_map/reduce_scatter | solution.py:29
  778.0 0.0 copy-start.6
  778.1 1.9 fusion.9
  779.9 0.0 copy-done.4
  779.9 0.0 copy-done.5
  779.9 0.0 copy-done.7
  779.9 2.8 fusion.5
  782.7 0.0 all-gather.8.cloned.1.call-update
  782.8 0.0 copy-done.6
  782.8 5.2 all-gather.2
  788.0 0.0 copy-done.3
  788.0 0.4 fusion.2
  788.5 0.0 copy-done.1
  788.5 0.0 copy-start.2
  788.5 0.7 fusion.6
  789.2 0.0 copy-start.8
  789.2 1.1 stack.2
  790.3 0.0 copy-done.2
  790.3 3.7 all-to-all-start
  794.0 0.0 copy-done.8
  794.1 0.6 fusion.22
  794.7 13.8 %all-to-all-done = f32[4,128,512]{2,1,0:T(8,128)S(1)} async-done(((f32[4,128,512]{2,1,0:T(8,128)}), f32[4,128,512]{2,1,0:T(8,128)S(1)}, u32[]{:S(2)}, u32[]{:S(2)}) %all-to-all-start) | async-done | bytes 1048608 | tf_op jit(solution)/shard_map/all_to_all | solution.py:53
  808.5 2.4 select_reduce_fusion
  811.6 0.1 broadcast_multiply_fusion
  811.7 1.9 fusion.1
  813.6 1.9 fusion.31
  815.5 1.9 fusion
  817.3 1.9 fusion.32
  819.2 1.4 fusion.4
  820.6 85.8 %all-gather.8.cloned.1.call-done = f32[1024,512]{1,0:T(8,128)} async-done(((f32[8,512]{1,0:T(8,128)}), f32[1024,512]{1,0:T(8,128)}) %all-gather.8.cloned.1.call-update) | async-done | bytes 2097168 | tf_op jit(solution)/shard_map/all_gather | solution.py:41
  906.4 2.3 gather_fusion.1
  908.7 1.5 broadcast_select_fusion
  (6 shorter events, 0.0 us)
Async XLA Ops:
  8.0 1.6 copy-start
  8.0 33.3 %all-gather.6.cloned.1.call-start = ((), (), s32[]{:S(2)}) async-start(), calls=%async_computation.3 | async-start | bytes 1310720 | tf_op jit(solution)/shard_map/all_gather | solution.py:32
  8.7 769.3 %reduce-scatter.2.cloned.1.call-start = ((), (), s32[]{:S(2)}) async-start(), calls=%async_computation.2 | async-start | bytes 2113536 | tf_op jit(solution)/shard_map/reduce_scatter | solution.py:29
  11.8 768.1 %copy-start.4 = (f32[1,8,512]{2,1,0:T(8,128)S(1)}, f32[1,8,512]{2,1,0:T(8,128)}, u32[]{:S(2)}) copy-start(f32[1,8,512]{2,1,0:T(8,128)} %param.9) | copy-start | bytes 49156
  11.8 768.1 %copy-start.5 = (f32[1,8,512]{2,1,0:T(8,128)S(1)}, f32[1,8,512]{2,1,0:T(8,128)}, u32[]{:S(2)}) copy-start(f32[1,8,512]{2,1,0:T(8,128)} %param.10) | copy-start | bytes 49156
  11.8 768.1 %copy-start.7 = (f32[1,8,512]{2,1,0:T(8,128)S(1)}, f32[1,8,512]{2,1,0:T(8,128)}, u32[]{:S(2)}) copy-start(f32[1,8,512]{2,1,0:T(8,128)} %param.8) | copy-start | bytes 49156
  11.8 776.2 %copy-start.3 = (f32[1,128,512]{2,1,0:T(8,128)S(1)}, f32[1,128,512]{2,1,0:T(8,128)}, u32[]{:S(2)}) copy-start(f32[1,128,512]{2,1,0:T(8,128)} %param.12) | copy-start | bytes 786436
  11.8 894.6 %all-gather.8.cloned.1.call-start = ((), (), s32[]{:S(2)}) async-start(), calls=%async_computation.4 | async-start | bytes 2113536 | tf_op jit(solution)/shard_map/all_gather | solution.py:41
  41.3 747.2 %copy-start.1 = (f32[1,512,512]{2,1,0:T(8,128)S(1)}, f32[1,512,512]{2,1,0:T(8,128)}, u32[]{:S(2)}) copy-start(f32[1,512,512]{2,1,0:T(8,128)} %all-gather.6.cloned.1.call-done) | copy-start | bytes 3145732
  778.0 4.7 copy-start.6
  788.5 1.8 copy-start.2
  789.2 4.8 copy-start.8
  790.3 18.1 %all-to-all-start = ((f32[4,128,512]{2,1,0:T(8,128)}), f32[4,128,512]{2,1,0:T(8,128)S(1)}, u32[]{:S(2)}, u32[]{:S(2)}) async-start(f32[4,128,512]{2,1,0:T(8,128)} %stack.2), calls=%async_computation.1 | async-start | bytes 2097152 | tf_op jit(solution)/shard_map/all_to_all | solution.py:53
Sparse Core Ops, SparseCore 0:
  10.9 30.3 all-gather.5
Sparse Core Ops, SparseCore 1:
  12.6 765.4 reduce-scatter.1
  782.8 123.5 all-gather.7
